TPU v7x, 512 devices: a whole 4x4x16 slice. The times are simulated.
512 devices in a mesh: page: 16 (over z), blk: 32 (over y, x, core).
Axes of the slice: x: 4, y: 4, z: 16, core: 2. Of those that a mesh axis runs over, the one named last changes fastest.
Arguments:
- queries: bfloat16 [64, 2, 32, 128], P(None, None, 'blk'), may hold values from -192 to 192
- prompt_kv: bfloat16 [256, 64, 32, 256], P('page', None, 'blk'), may hold values from -36 to 36
- tail_kv: bfloat16 [64, 256, 32, 256], P('page', None, 'blk'), may hold values from -36 to 36
- page_table: int32 [4, 64], replicated, may hold values from 0 to 255, as said below
- prompt_len: int32 [4], replicated, may hold values from 1 to 4096, 10240 in all
- tail_len: int32 [64], replicated, may hold values from 0 to 254, as said below
- sample_prompt: int32 [64], replicated, may hold values from 0 to 3, as said below
- stream_in: bfloat16 [64, 2, 7168], P(None, None, 'blk'), may hold values from -6 to 6
- w_out: bfloat16 [4096, 7168], P('blk'), may hold values from -0.09375 to 0.09375
- b_out: bfloat16 [7168], replicated, may hold values from -3 to 3
- ln_gain: bfloat16 [7168], P('page'), may hold values from 0.25 to 1.75
- ln_bias: bfloat16 [7168], P('page'), may hold values from -3 to 3
- w_up: bfloat16 [7168, 28672], P('page', 'blk'), may hold values from -0.0625 to 0.0625
- b_up: bfloat16 [28672], P('blk'), may hold values from -3 to 3
- w_down: bfloat16 [28672, 7168], P('blk', 'page'), may hold values from -0.046875 to 0.046875
- b_down: bfloat16 [7168], P(('page', 'blk')), may hold values from -3 to 3
- w_score: bfloat16 [7168], P(('page', 'blk')), may hold values from -0.0625 to 0.0625
Outputs:
- layer_output: bfloat16 [64, 2, 7168], P(None, None, ('page', 'blk'))
- sample_score: float32 [64, 2], replicated
Inputs may be any that keep to these rules, and one draw needn't show every extreme that they name: `page_table`: every slot number appears exactly once in the table. `tail_len`: some sample reaches the largest value. `sample_prompt`: each prompt has exactly 16 samples.
All inputs are finite; a program needn't handle non-finite values.
Results may differ from a plain program's by a relative error of at most 0.03.
Values may be sent and summed in bfloat16 or wider, within the bound.
A program may use at most 64 MiB of HBM per device.

v0:
```python
import math
import jax
import jax.numpy as jnp
from jax import lax
from jax.sharding import PartitionSpec as P

NEGATIVE = -1e30


def combined_all(value, axis, join):
    pieces = jax.tree.map(lambda part: lax.all_gather(part, axis), value)
    head = jax.tree.map(lambda part: part[0], pieces)
    tail = jax.tree.map(lambda part: part[1:], pieces)
    subtotal, _ = lax.scan(lambda subtotal, share: (join(subtotal, share), None), head, tail)
    return subtotal


def join_partials(earlier, later):
    highest = jnp.maximum(earlier[0], later[0])
    left_scale = jnp.exp(earlier[0] - highest)
    right_scale = jnp.exp(later[0] - highest)
    return (
        highest,
        earlier[1] * left_scale + later[1] * right_scale,
        earlier[2] * left_scale[..., None] + later[2] * right_scale[..., None],
    )


def softmax_part(scores, visible):
    masked = jnp.where(visible, scores, NEGATIVE)
    highest = jnp.max(masked, axis=-1)
    weights = jnp.where(visible, jnp.exp(scores - highest[..., None]), 0.0)
    return (highest, jnp.sum(weights, axis=-1), weights.astype(jnp.bfloat16))


def body(
    queries,
    prompt_kv,
    tail_kv,
    page_table,
    prompt_len,
    tail_len,
    sample_prompt,
    stream_in,
    w_out,
    b_out,
    ln_gain,
    ln_bias,
    w_up,
    b_up,
    w_down,
    b_down,
    w_score,
):
    samples, new_count, heads_dev, head_dim = queries.shape
    slots_dev, page_len = (prompt_kv.shape[0], prompt_kv.shape[1])
    own_count, tail_max = (tail_kv.shape[0], tail_kv.shape[1])
    prompts, pages_max = page_table.shape
    page_pos = lax.axis_index("page")
    blk_pos = lax.axis_index("blk")
    inv_sqrt = 1.0 / math.sqrt(head_dim)
    entries = page_table.reshape(-1)
    slot_ids = page_pos * slots_dev + jnp.arange(slots_dev, dtype=jnp.int32)
    matched = (entries[:, None] == slot_ids[None, :]).astype(jnp.int32)
    owner_index = jnp.sum(matched * jnp.arange(entries.shape[0], dtype=jnp.int32)[:, None], axis=0)
    slot_prompt = owner_index // pages_max
    slot_page = owner_index % pages_max
    prompt_pick = (slot_prompt[:, None] == jnp.arange(prompts, dtype=jnp.int32)[None, :]).astype(
        jnp.int32
    )
    slot_limit = jnp.sum(prompt_pick * prompt_len[None, :], axis=1)
    key_pos = slot_page[:, None] * page_len + jnp.arange(page_len, dtype=jnp.int32)[None, :]
    key_live = (key_pos < slot_limit[:, None]).reshape(-1)
    key_prompt = jnp.repeat(slot_prompt, page_len)
    prompt_visible = ((sample_prompt[:, None] == key_prompt[None, :]) & key_live[None, :])[
        :, None, None, :
    ]
    cache_rows = prompt_kv.reshape(slots_dev * page_len, heads_dev, 2 * head_dim)
    prompt_scores = (
        jnp.einsum(
            "snhd,khd->snhk",
            queries,
            cache_rows[:, :, :head_dim],
            preferred_element_type=jnp.float32,
        )
        * inv_sqrt
    )
    high_p, sum_p, weights_p = softmax_part(prompt_scores, prompt_visible)
    mixed_p = jnp.einsum(
        "snhk,khd->snhd", weights_p, cache_rows[:, :, head_dim:], preferred_element_type=jnp.float32
    )
    first_row = page_pos * own_count
    own_queries = lax.dynamic_slice_in_dim(queries, first_row, own_count, 0)
    own_lengths = lax.dynamic_slice_in_dim(tail_len, first_row, own_count, 0)
    tail_scores = (
        jnp.einsum(
            "snhd,sthd->snht",
            own_queries,
            tail_kv[..., :head_dim],
            preferred_element_type=jnp.float32,
        )
        * inv_sqrt
    )
    reach_pos = own_lengths[:, None] + jnp.arange(new_count, dtype=jnp.int32)[None, :]
    tail_visible = (
        jnp.arange(tail_max, dtype=jnp.int32)[None, None, None, :] <= reach_pos[:, :, None, None]
    )
    high_t, sum_t, weights_t = softmax_part(tail_scores, tail_visible)
    mixed_t = jnp.einsum(
        "snht,sthd->snhd", weights_t, tail_kv[..., head_dim:], preferred_element_type=jnp.float32
    )
    high_t = lax.dynamic_update_slice_in_dim(
        jnp.full(high_p.shape, NEGATIVE, jnp.float32), high_t, first_row, 0
    )
    sum_t = lax.dynamic_update_slice_in_dim(
        jnp.zeros(sum_p.shape, jnp.float32), sum_t, first_row, 0
    )
    mixed_t = lax.dynamic_update_slice_in_dim(
        jnp.zeros(mixed_p.shape, jnp.float32), mixed_t, first_row, 0
    )
    partial_value = join_partials((high_p, sum_p, mixed_p), (high_t, sum_t, mixed_t))
    merged = combined_all(partial_value, "page", join_partials)
    weight_sum, weighted = (merged[1], merged[2])
    attention = (
        (weighted / weight_sum[..., None])
        .astype(jnp.bfloat16)
        .reshape(samples * new_count, heads_dev * head_dim)
    )
    contrib = jnp.dot(attention, w_out, preferred_element_type=jnp.float32)
    slice_width = stream_in.shape[2]
    column = blk_pos * slice_width
    own_stream = stream_in.reshape(samples * new_count, slice_width).astype(jnp.float32)
    contrib = lax.dynamic_update_slice_in_dim(
        contrib, lax.dynamic_slice_in_dim(contrib, column, slice_width, 1) + own_stream, column, 1
    )
    summed = lax.psum(contrib, "blk")
    residual = (summed + b_out.astype(jnp.float32)).astype(jnp.bfloat16)
    residual_f = residual.astype(jnp.float32)
    row_mean = jnp.mean(residual_f, axis=-1, keepdims=True)
    centred = residual_f - row_mean
    inverse_std = lax.rsqrt(jnp.mean(centred * centred, axis=-1, keepdims=True) + 1e-05)
    feature_count = ln_gain.shape[0]
    first_col = page_pos * feature_count
    normed = (
        lax.dynamic_slice_in_dim(centred, first_col, feature_count, 1)
        * inverse_std
        * ln_gain.astype(jnp.float32)
        + ln_bias.astype(jnp.float32)
    ).astype(jnp.bfloat16)
    up_part = jnp.dot(normed, w_up, preferred_element_type=jnp.float32).astype(jnp.bfloat16)
    hidden_sum = lax.psum(up_part, "page").astype(jnp.float32)
    hidden = jnp.maximum(hidden_sum + b_up.astype(jnp.float32), 0.0).astype(jnp.bfloat16)
    projected = jnp.dot(hidden, w_down, preferred_element_type=jnp.float32)
    out_share = lax.psum_scatter(projected, "blk", scatter_dimension=1, tiled=True)
    piece_width = b_down.shape[0]
    out_column = first_col + blk_pos * piece_width
    output = (
        out_share
        + lax.dynamic_slice_in_dim(residual_f, out_column, piece_width, 1)
        + b_down.astype(jnp.float32)
    ).astype(jnp.bfloat16)
    score_part = jnp.sum(output.astype(jnp.float32) * w_score.astype(jnp.float32), axis=-1)
    row_score = lax.psum(score_part, ("page", "blk"))
    return (output.reshape(samples, new_count, piece_width), row_score.reshape(samples, new_count))


def solution(mesh):
    placed = (
        P(None, None, "blk", None),
        P("page", None, "blk", None),
        P("page", None, "blk", None),
        P(),
        P(),
        P(),
        P(),
        P(None, None, "blk"),
        P("blk", None),
        P(),
        P("page"),
        P("page"),
        P("page", "blk"),
        P("blk"),
        P("blk", "page"),
        P(("page", "blk")),
        P(("page", "blk")),
    )
    return jax.shard_map(
        body,
        mesh=mesh,
        in_specs=placed,
        out_specs=(P(None, None, ("page", "blk")), P()),
        check_vma=False,
    )
```

profile of v0, /device:TPU:1, one launch (start us, length us, event | category | flops | bytes accessed | tf_op | source)
XLA Modules:
  0.0 637.5 jit_solution(366933933234473874)
XLA Ops:
  7.2 0.9 dynamic_slice.26
  8.2 1.2 select_reduce_fusion.2
  9.7 1.2 fusion.14
  10.9 0.8 eq.50
  11.9 0.7 select_reduce_fusion.3
  13.2 0.8 compare_and_fusion
  14.0 1.3 select_reduce_fusion
  15.2 0.3 fusion.11
  15.5 1.9 fusion.8
  17.6 33.1 %all-gather = f32[1024,2,1]{1,2,0:T(1,128)S(1)} all-gather(f32[64,2,1]{1,2,0:T(1,128)S(1)} %copy.76), channel_id=2, replica_groups=mesh['page'=16,'blk'=32] {'page'}, dimensions={0}, use_global_device_ids=true | all-gather | bytes 8704 | tf_op jit(solution)/shard_map/all_gather | solution.py:11
  50.9 25.1 %all-gather.1 = f32[1024,2,1]{1,2,0:T(1,128)S(1)} all-gather(f32[64,2,1]{1,2,0:T(1,128)S(1)} %copy.78), channel_id=3, replica_groups=mesh['page'=16,'blk'=32] {'page'}, dimensions={0}, use_global_device_ids=true | all-gather | bytes 8704 | tf_op jit(solution)/shard_map/all_gather | solution.py:11
  76.2 0.2 copy.87
  76.7 8.9 %all-gather.5.cloned.1.call-done = f32[1024,2,1,128]{3,0,1,2:T(8,128)} async-done(((f32[64,2,1,128]{3,0,1,2:T(8,128)}), f32[1024,2,1,128]{3,0,1,2:T(8,128)}) %all-gather.5.cloned.1.call-update) | async-done | bytes 1048592 | tf_op jit(solution)/shard_map/all_gather | solution.py:11
  85.6 0.8 slice.52
  86.5 1.3 slice.55
  87.7 10.6 %while.14 = (s32[]{:T(128)}, f32[64,2,1]{0,1,2:T(2,128)S(1)}, f32[64,2,1]{0,1,2:T(2,128)S(1)}, f32[64,2,1,128]{3,2,1,0:T(1,128)S(1)}, f32[15,64,2,1]{1,2,3,0:T(2...) while((s32[]{:T(128)}, f32[64,2,1]{0,1,2:T(2,128)S(1)}, ...), condition=%wide.region_7.8_spmd, body=%wide.region_6.7_spmd.sunk | while | flops 50050 | bytes 468577 | solution.py:14
  88.1 0.4 multiply_add_fusion.2
  88.8 0.4 multiply_add_fusion.2
  89.5 0.4 multiply_add_fusion.2
  90.2 0.4 multiply_add_fusion.2
  90.9 0.4 multiply_add_fusion.2
  91.6 0.4 multiply_add_fusion.2
  92.3 0.4 multiply_add_fusion.2
  93.0 0.4 multiply_add_fusion.2
  93.7 0.4 multiply_add_fusion.2
  94.4 0.4 multiply_add_fusion.2
  95.1 0.4 multiply_add_fusion.2
  95.8 0.4 multiply_add_fusion.2
  96.5 0.4 multiply_add_fusion.2
  97.2 0.4 multiply_add_fusion.2
  97.9 0.4 multiply_add_fusion.2
  98.4 0.2 divide_convert_fusion
  98.7 0.6 fusion.44
  99.4 1.8 copy-done.1
  101.3 1.9 dynamic_update_slice.15
  103.3 147.2 %all-reduce.5.cloned.1.call-done = f32[128,7168]{1,0:T(8,128)} async-done(((f32[128,7168]{1,0:T(8,128)}), f32[128,7168]{1,0:T(8,128)}) %all-reduce.5.cloned.1.call-update) | async-done | bytes 3670032 | tf_op jit(solution)/shard_map/psum | solution.py:136
  250.5 2.5 fusion.42
  253.1 0.8 multiply_reduce_fusion
  253.9 1.0 copy-done.2
  254.9 1.1 convolution_convert_fusion
  256.1 126.2 %all-reduce.7.cloned.1.call-done = bf16[128,896]{1,0:T(8,128)(2,1)} async-done(((bf16[128,896]{1,0:T(8,128)(2,1)}), bf16[128,896]{1,0:T(8,128)(2,1)}) %all-reduce.7.cloned.1.call-update) | async-done | bytes 229392 | tf_op jit(solution)/shard_map/psum | solution.py:151
  382.3 2.0 fusion.18
  384.4 1.3 dynamic-slice
  386.3 137.0 %all-reduce.9.cloned.1.call-done = f32[128,448]{1,0:T(8,128)} async-done(((f32[128,448]{1,0:T(8,128)}), f32[128,448]{1,0:T(8,128)}) %all-reduce.9.cloned.1.call-update) | async-done | bytes 229392
  523.3 1.1 multiply_reduce_fusion.1
  524.6 105.0 %psum.23 = f32[64,2]{1,0:T(8,128)S(1)} all-reduce(f32[64,2]{1,0:T(8,128)S(1)} %reshape.251), channel_id=1, replica_groups=mesh['page'=16,'blk'=32] {'page','blk'}, use_global_device_ids=true, to_apply=%region_14.15 | all-reduce | flops 128 | bytes 1024 | tf_op jit(solution)/shard_map/psum | solution.py:163
  629.6 0.6 copy.92
  630.3 0.7 copy.91
  (176 shorter events, 7.0 us)
Async XLA Ops:
  7.2 91.5 %copy-start = (bf16[128,7168]{1,0:T(8,128)(2,1)S(1)}, bf16[128,7168]{1,0:T(8,128)(2,1)}, u32[]{:S(2)}) copy-start(bf16[128,7168]{1,0:T(8,128)(2,1)} %param.27) | copy-start | bytes 5505028
  7.2 78.4 %all-gather.5.cloned.1.call-start = ((), (), s32[]{:S(2)}) async-start(), calls=%async_computation.2 | async-start | bytes 1114112 | tf_op jit(solution)/shard_map/all_gather | solution.py:11
  12.7 63.9 %copy-start.5 = (bf16[64,2,224]{2,1,0:T(2,128)(2,1)S(1)}, bf16[64,2,224]{2,1,0:T(2,128)(2,1)}, u32[]{:S(2)}) copy-start(bf16[64,2,224]{2,1,0:T(2,128)(2,1)} %param.26) | copy-start | bytes 172036
  17.4 233.1 %all-reduce.5.cloned.1.call-start = ((), (), s32[]{:S(2)}) async-start(), calls=%async_computation | async-start | bytes 7340032 | tf_op jit(solution)/shard_map/psum | solution.py:136
  98.7 4.6 copy-start.6
  98.7 4.6 copy-start.8
  98.7 4.6 copy-start.9
  99.3 1.8 copy-start.1
  103.2 279.1 %all-reduce.7.cloned.1.call-start = ((), (), s32[]{:S(2)}) async-start(), calls=%async_computation.1 | async-start | bytes 458752 | tf_op jit(solution)/shard_map/psum | solution.py:151
  253.0 1.9 copy-start.2
  253.1 1.9 copy-start.4
  253.1 3.0 copy-start.7
  253.1 129.2 %copy-start.3 = (bf16[896,448]{0,1:T(8,128)(2,1)S(1)}, bf16[896,448]{0,1:T(8,128)(2,1)}, u32[]{:S(2)}) copy-start(bf16[896,448]{0,1:T(8,128)(2,1)} %param.33) | copy-start | bytes 2408452
  253.1 131.3 %copy-start.10 = (bf16[14]{0:T(256)(128)(2,1)S(1)}, bf16[14]{0:T(256)(128)(2,1)}, u32[]{:S(2)}) copy-start(bf16[14]{0:T(256)(128)(2,1)} %param.34) | copy-start | bytes 88
  253.1 131.3 %copy-start.11 = (bf16[14]{0:T(256)(128)(2,1)S(1)}, bf16[14]{0:T(256)(128)(2,1)}, u32[]{:S(2)}) copy-start(bf16[14]{0:T(256)(128)(2,1)} %param.35) | copy-start | bytes 88
  256.0 267.3 %all-reduce.9.cloned.1.call-start = ((), (), s32[]{:S(2)}) async-start(), calls=%async_computation.3 | async-start | bytes 524288
Sparse Core Ops, SparseCore 0:
  17.6 67.9 all-gather.4
  103.3 147.1 all-reduce.4
  256.2 126.0 all-reduce.6
  385.7 137.5 all-reduce.8
where the time goes:
time: 638 us; the launch traced here: 637 us
  waiting for transfers between devices  419 us (66%)
  blocking collectives  163 us (26%)
  local copies, waits for them, and re-layouts  16.8 us (3%)
  between operations  14.8 us (2%)
  other arithmetic  13.4 us (2%)
  matrix products  9.27 us (1%)
    psum x1, waiting for transfers between devices, body(): summed = lax.psum(contrib, 'blk')  147 us
    unnamed x5, waiting for transfers between devices  137 us
    psum x1, waiting for transfers between devices, body(): hidden_sum = lax.psum(up_part, 'page').astype(jnp.float32)  126 us
    psum x1, blocking collectives, body(): row_score = lax.psum(score_part, ('page', 'blk'))  105 us
    all_gather x2, blocking collectives, combined_all(): pieces = jax.tree.map(lambda part: lax.all_gather(part, axis), value)  58.2 us
  transfers between devices with their start and end apart: 4, of which 4 were waited for; matrix products, arithmetic and copies ran while one was open for 0% of the time, Pallas kernels for 0%

commit v1 on v0

--- a/solution.py
+++ b/solution.py
@@ -148,7 +148,7 @@
         + ln_bias.astype(jnp.float32)
     ).astype(jnp.bfloat16)
     up_part = jnp.dot(normed, w_up, preferred_element_type=jnp.float32).astype(jnp.bfloat16)
-    hidden_sum = lax.psum(up_part, "page").astype(jnp.float32)
+    hidden_sum = jnp.sum(jax.lax.all_gather(up_part, axis_name="page"), 0).astype(jnp.float32)
     hidden = jnp.maximum(hidden_sum + b_up.astype(jnp.float32), 0.0).astype(jnp.bfloat16)
     projected = jnp.dot(hidden, w_down, preferred_element_type=jnp.float32)
     out_share = lax.psum_scatter(projected, "blk", scatter_dimension=1, tiled=True)

time: 638 us -> 581 us (0.911)
  waiting for transfers between devices: 419 us -> 361 us
    psum x1 -> x0, waiting for transfers between devices: 126 us -> none  [body(): hidden_sum = lax.psum(up_part, 'page').astype(jnp.float32)]
    all_gather x0 -> x1, waiting for transfers between devices: none -> 69 us  [body(): jax.lax.all_gather(up_part, axis_name='page')]
where the time goes in v1:
time: 581 us; the launch traced here: 580 us
  waiting for transfers between devices  361 us (62%)
  blocking collectives  163 us (28%)
  local copies, waits for them, and re-layouts  16.7 us (3%)
  other arithmetic  16 us (3%)
  between operations  14.8 us (3%)
  matrix products  8.33 us (1%)
    psum x1, waiting for transfers between devices, body(): summed = lax.psum(contrib, 'blk')  147 us
    unnamed x5, waiting for transfers between devices  136 us
    psum x1, blocking collectives, body(): row_score = lax.psum(score_part, ('page', 'blk'))  105 us
    all_gather x1, waiting for transfers between devices, body(): jax.lax.all_gather(up_part, axis_name='page')  69 us
    all_gather x2, blocking collectives, combined_all(): pieces = jax.tree.map(lambda part: lax.all_gather(part, axis), value)  58.2 us
  transfers between devices with their start and end apart: 4, of which 4 were waited for; matrix products, arithmetic and copies ran while one was open for 0% of the time, Pallas kernels for 0%

profile of v1, /device:TPU:1, one launch (start us, length us, event | category | flops | bytes accessed | tf_op | source)
XLA Modules:
  0.0 580.4 jit_solution(5242662359437724192)
XLA Ops:
  7.2 0.9 dynamic_slice.26
  8.2 1.2 select_reduce_fusion.2
  9.7 1.2 fusion.14
  10.9 0.8 eq.50
  11.9 0.7 select_reduce_fusion.3
  13.2 0.8 compare_and_fusion
  14.0 1.3 select_reduce_fusion
  15.2 0.3 fusion.11
  15.5 1.9 fusion.8
  17.6 33.1 %all-gather = f32[1024,2,1]{1,2,0:T(1,128)S(1)} all-gather(f32[64,2,1]{1,2,0:T(1,128)S(1)} %copy.76), channel_id=2, replica_groups=mesh['page'=16,'blk'=32] {'page'}, dimensions={0}, use_global_device_ids=true | all-gather | bytes 8704 | tf_op jit(solution)/shard_map/all_gather | solution.py:11
  50.9 25.1 %all-gather.1 = f32[1024,2,1]{1,2,0:T(1,128)S(1)} all-gather(f32[64,2,1]{1,2,0:T(1,128)S(1)} %copy.78), channel_id=3, replica_groups=mesh['page'=16,'blk'=32] {'page'}, dimensions={0}, use_global_device_ids=true | all-gather | bytes 8704 | tf_op jit(solution)/shard_map/all_gather | solution.py:11
  76.2 0.2 copy.87
  76.7 8.9 %all-gather.7.cloned.1.call-done = f32[1024,2,1,128]{3,0,1,2:T(8,128)} async-done(((f32[64,2,1,128]{3,0,1,2:T(8,128)}), f32[1024,2,1,128]{3,0,1,2:T(8,128)}) %all-gather.7.cloned.1.call-update) | async-done | bytes 1048592 | tf_op jit(solution)/shard_map/all_gather | solution.py:11
  85.6 0.8 slice.52
  86.5 1.3 slice.55
  87.7 10.6 %while.14 = (s32[]{:T(128)}, f32[64,2,1]{0,1,2:T(2,128)S(1)}, f32[64,2,1]{0,1,2:T(2,128)S(1)}, f32[64,2,1,128]{3,2,1,0:T(1,128)S(1)}, f32[15,64,2,1]{1,2,3,0:T(2...) while((s32[]{:T(128)}, f32[64,2,1]{0,1,2:T(2,128)S(1)}, ...), condition=%wide.region_7.8_spmd, body=%wide.region_6.7_spmd.sunk | while | flops 50050 | bytes 468577 | solution.py:14
  88.1 0.4 multiply_add_fusion.2
  88.8 0.4 multiply_add_fusion.2
  89.5 0.4 multiply_add_fusion.2
  90.2 0.4 multiply_add_fusion.2
  90.9 0.4 multiply_add_fusion.2
  91.6 0.4 multiply_add_fusion.2
  92.3 0.4 multiply_add_fusion.2
  93.0 0.4 multiply_add_fusion.2
  93.7 0.4 multiply_add_fusion.2
  94.4 0.4 multiply_add_fusion.2
  95.1 0.4 multiply_add_fusion.2
  95.8 0.4 multiply_add_fusion.2
  96.5 0.4 multiply_add_fusion.2
  97.2 0.4 multiply_add_fusion.2
  97.9 0.4 multiply_add_fusion.2
  98.7 0.6 fusion.44
  99.4 1.8 copy-done.1
  101.3 1.9 dynamic_update_slice.15
  103.3 147.2 %all-reduce.4.cloned.1.call-done = f32[128,7168]{1,0:T(8,128)} async-done(((f32[128,7168]{1,0:T(8,128)}), f32[128,7168]{1,0:T(8,128)}) %all-reduce.4.cloned.1.call-update) | async-done | bytes 3670032 | tf_op jit(solution)/shard_map/psum | solution.py:136
  250.5 2.5 fusion.42
  253.1 0.8 multiply_reduce_fusion
  253.9 1.0 copy-done.2
  254.9 1.1 convolution_convert_fusion
  256.0 69.0 %all-gather.9.cloned.1.call-done = bf16[2048,896]{1,0:T(8,128)(2,1)} async-done(((bf16[128,896]{1,0:T(8,128)(2,1)}), bf16[2048,896]{1,0:T(8,128)(2,1)}) %all-gather.9.cloned.1.call-update) | async-done | bytes 3670032 | tf_op jit(solution)/shard_map/all_gather | solution.py:151
  325.0 2.6 reduce_sum.87
  327.6 1.1 fusion.18
  328.8 1.3 dynamic-slice
  330.7 135.5 %all-reduce.6.cloned.1.call-done = f32[128,448]{1,0:T(8,128)} async-done(((f32[128,448]{1,0:T(8,128)}), f32[128,448]{1,0:T(8,128)}) %all-reduce.6.cloned.1.call-update) | async-done | bytes 229392
  466.3 1.1 multiply_reduce_fusion.1
  467.6 105.0 %psum.15 = f32[64,2]{1,0:T(8,128)S(1)} all-reduce(f32[64,2]{1,0:T(8,128)S(1)} %reshape.251), channel_id=1, replica_groups=mesh['page'=16,'blk'=32] {'page','blk'}, use_global_device_ids=true, to_apply=%region_14.15 | all-reduce | flops 128 | bytes 1024 | tf_op jit(solution)/shard_map/psum | solution.py:163
  572.6 0.6 copy.92
  573.2 0.7 copy.91
  (177 shorter events, 7.2 us)
Async XLA Ops:
  7.2 91.5 %copy-start = (bf16[128,7168]{1,0:T(8,128)(2,1)S(1)}, bf16[128,7168]{1,0:T(8,128)(2,1)}, u32[]{:S(2)}) copy-start(bf16[128,7168]{1,0:T(8,128)(2,1)} %param.27) | copy-start | bytes 5505028
  7.2 78.4 %all-gather.7.cloned.1.call-start = ((), (), s32[]{:S(2)}) async-start(), calls=%async_computation.1 | async-start | bytes 1114112 | tf_op jit(solution)/shard_map/all_gather | solution.py:11
  12.7 63.9 %copy-start.5 = (bf16[64,2,224]{2,1,0:T(2,128)(2,1)S(1)}, bf16[64,2,224]{2,1,0:T(2,128)(2,1)}, u32[]{:S(2)}) copy-start(bf16[64,2,224]{2,1,0:T(2,128)(2,1)} %param.26) | copy-start | bytes 172036
  17.4 233.1 %all-reduce.4.cloned.1.call-start = ((), (), s32[]{:S(2)}) async-start(), calls=%async_computation | async-start | bytes 7340032 | tf_op jit(solution)/shard_map/psum | solution.py:136
  98.7 4.6 copy-start.6
  98.7 4.6 copy-start.8
  98.7 4.6 copy-start.9
  99.3 1.8 copy-start.1
  103.2 221.8 %all-gather.9.cloned.1.call-start = ((), (), s32[]{:S(2)}) async-start(), calls=%async_computation.2 | async-start | bytes 3899392 | tf_op jit(solution)/shard_map/all_gather | solution.py:151
  253.0 1.8 copy-start.2
  253.1 1.8 copy-start.4
  253.1 2.9 copy-start.7
  254.9 72.8 %copy-start.3 = (bf16[896,448]{0,1:T(8,128)(2,1)S(1)}, bf16[896,448]{0,1:T(8,128)(2,1)}, u32[]{:S(2)}) copy-start(bf16[896,448]{0,1:T(8,128)(2,1)} %param.33) | copy-start | bytes 2408452
  254.9 73.9 %copy-start.10 = (bf16[14]{0:T(256)(128)(2,1)S(1)}, bf16[14]{0:T(256)(128)(2,1)}, u32[]{:S(2)}) copy-start(bf16[14]{0:T(256)(128)(2,1)} %param.34) | copy-start | bytes 88
  254.9 73.9 %copy-start.11 = (bf16[14]{0:T(256)(128)(2,1)S(1)}, bf16[14]{0:T(256)(128)(2,1)}, u32[]{:S(2)}) copy-start(bf16[14]{0:T(256)(128)(2,1)} %param.35) | copy-start | bytes 88
  256.0 210.3 %all-reduce.6.cloned.1.call-start = ((), (), s32[]{:S(2)}) async-start(), calls=%async_computation.3 | async-start | bytes 524288
Sparse Core Ops, SparseCore 0:
  17.6 67.9 all-gather.6
  103.3 147.1 all-reduce.3
  256.1 68.8 all-gather.8
  328.9 137.3 all-reduce.5
